TPU v7x, 32 devices: a whole 2x2x4 slice. The times are simulated.
32 devices in a mesh: wide: 8 (over y, x, core), narrow: 4 (over z).
Axes of the slice: x: 2, y: 2, z: 4, core: 2. Of those that a mesh axis runs over, the one named last changes fastest.
Arguments:
- events: bfloat16 [8192, 1024], P('wide'), may hold values from -36 to 36
- lengths: int32 [24], replicated, may hold values from 1 to 2048, 8192 in all
- in_gain: float32 [1024], replicated, may hold values from 0.1 to 1.9
- w_uvqk: bfloat16 [1024, 8, 512], P(None, 'narrow'), may hold values from -2 to 2, as said below
- out_gain: float32 [8, 128], P('narrow'), may hold values from 0.1 to 1.9
- w_out: bfloat16 [8, 128, 1024], P('narrow'), may hold values from -0.25 to 0.25
Outputs:
- layer_out: bfloat16 [8192, 1024], P('wide', 'narrow')
Inputs may be any that keep to these rules, and one draw needn't show every extreme that they name: `w_uvqk`: projection weights.
All inputs are finite; a program needn't handle non-finite values.
Results may differ from a plain program's by a relative error of at most 0.0036.
Values may be sent and summed in bfloat16 or wider, within the bound.
A program may use at most 64 MiB of HBM per device.

v0:
```python
import jax
import jax.numpy as jnp
from jax import lax
from jax.sharding import PartitionSpec as P


def from_behind(value, axis, steps):
    count = lax.axis_size(axis)
    initial, last = (max(0, -steps), min(count, count - steps))
    return lax.ppermute(value, axis, [(source, source + steps) for source in range(initial, last)])


def fetch_relay(pair):
    return from_behind((pair[0], pair[1]), "wide", 1)


def on_device(events, lengths, in_gain, w_uvqk, out_gain, w_out):
    rows_w = events.shape[0]
    heads_local = w_uvqk.shape[1]
    head_size = out_gain.shape[1]
    events_f = events.astype(jnp.float32)
    average = jnp.mean(events_f, axis=-1, keepdims=True)
    variance = jnp.mean((events_f - average) ** 2, axis=-1, keepdims=True)
    normed = ((events_f - average) * lax.rsqrt(variance + 1e-05) * in_gain).astype(jnp.bfloat16)
    projected = jnp.einsum("rd,dhc->rhc", normed, w_uvqk, preferred_element_type=jnp.float32)
    projected = jax.nn.silu(projected).astype(jnp.bfloat16)
    update_gate = projected[:, :, :head_size]
    values_own = projected[:, :, head_size : 2 * head_size]
    queries = projected[:, :, 2 * head_size : 3 * head_size]
    keys_own = projected[:, :, 3 * head_size :]
    user_ends = jnp.cumsum(lengths)

    def owner_of(grow):
        return jnp.sum((user_ends[None, :] <= grow[:, None]).astype(jnp.int32), axis=1)

    first_row = lax.axis_index("wide") * rows_w
    query_pos = first_row + jnp.arange(rows_w, dtype=jnp.int32)
    query_user = owner_of(query_pos)
    scaling = head_size ** (-0.5)

    def attend(running, key_rows, value_rows, key_first):
        key_count = key_rows.shape[0]
        block_rows = 512

        def block_step(carry, block_index):
            key_start = block_index * block_rows
            key_block = lax.dynamic_slice_in_dim(key_rows, key_start, block_rows, 0)
            value_block = lax.dynamic_slice_in_dim(value_rows, key_start, block_rows, 0)
            key_pos = key_first + key_start + jnp.arange(block_rows, dtype=jnp.int32)
            key_user = owner_of(key_pos)
            allowed = (
                (key_user[None, :] == query_user[:, None])
                & (key_pos[None, :] <= query_pos[:, None])
                & (key_pos[None, :] >= 0)
            )
            scores = (
                jnp.einsum("rhc,khc->hrk", queries, key_block, preferred_element_type=jnp.float32)
                * scaling
            )
            weights = jnp.where(allowed[None], jax.nn.silu(scores), 0.0).astype(jnp.bfloat16)
            carry = carry + jnp.einsum(
                "hrk,khc->rhc", weights, value_block, preferred_element_type=jnp.float32
            )
            return (carry, None)

        running, _ = lax.scan(
            block_step, running, jnp.arange(key_count // block_rows, dtype=jnp.int32)
        )
        return running

    attended = attend(
        jnp.zeros((rows_w, heads_local, head_size), jnp.float32), keys_own, values_own, first_row
    )
    reach = lax.axis_size("wide") // 4

    def relay_turn(turn_index, carry):
        keys_held, values_held, running = carry
        keys_held, values_held = fetch_relay((keys_held, values_held))
        running = attend(running, keys_held, values_held, first_row - turn_index * rows_w)
        return (keys_held, values_held, running)

    _, _, attended = lax.fori_loop(1, reach + 1, relay_turn, (keys_own, values_own, attended))
    centre = jnp.mean(attended, axis=-1, keepdims=True)
    deviation = jnp.mean((attended - centre) ** 2, axis=-1, keepdims=True)
    gated = (
        (attended - centre)
        * lax.rsqrt(deviation + 1e-05)
        * out_gain[None]
        * update_gate.astype(jnp.float32)
    )
    gated = gated.astype(jnp.bfloat16)
    columns = lax.all_to_all(w_out, "narrow", split_axis=2, concat_axis=0, tiled=True)
    summed = jnp.einsum(
        "rhc,hcd->rd",
        lax.all_gather(gated, "narrow", axis=1, tiled=True),
        columns,
        preferred_element_type=jnp.float32,
    )
    share = summed.shape[1]
    own_cols = lax.dynamic_slice_in_dim(events_f, lax.axis_index("narrow") * share, share, 1)
    return (own_cols + summed).astype(jnp.bfloat16)


def solution(mesh):
    in_specs = (
        P("wide", None),
        P(),
        P(),
        P(None, "narrow", None),
        P("narrow", None),
        P("narrow", None, None),
    )
    out_specs = P("wide", "narrow")
    return jax.shard_map(
        on_device, mesh=mesh, in_specs=in_specs, out_specs=out_specs, check_vma=False
    )
```

profile of v0, /device:TPU:4, one launch (start us, length us, event | category | flops | bytes accessed | tf_op | source)
XLA Modules:
  0.0 164.0 jit_solution(15008756031488288233)
XLA Ops:
  6.6 2.1 %convert_reduce_fusion.2 = f32[1024]{0:T(1024)S(1)} fusion(bf16[1024,1024]{1,0:T(8,128)(2,1)} %param.12), kind=kLoop, calls=%fused_computation.47 | loop fusion | flops 2096128 | bytes 2101248 | tf_op jit(solution)/shard_map/reduce_sum | solution.py:22
  8.6 2.3 %multiply_reduce_fusion = f32[1024]{0:T(1024)S(1)} fusion(bf16[1024,1024]{1,0:T(8,128)(2,1)} %param.12, f32[1024]{0:T(1024)S(1)} %broadcast_multiply_fusion.1), kind=kLoop, calls=%fused_computation.46 | loop fusion | flops 4193280 | bytes 2105344 | tf_op jit(solution)/shard_map/reduce_sum | solution.py:23
  11.0 3.4 %multiply_convert_fusion = bf16[1024,2,512]{2,0,1:T(8,128)(2,1)S(1)} fusion(bf16[1024,2,512]{2,1,0:T(2,128)(2,1)S(1)} %copy-done, bf16[1024,1024]{1,0:T(8,128)(2,1)S(1)} %copy-done.1, f32[1024]{0:T(1024)S(1)} %copy-done.5, f32[1024]{0:T(1024)S(1)} %add_rsqrt_fusion.1, f32[1024]{0:T(1024)S(1)} %broadcast_multiply_fusion.1), kind=kOutput, calls=%fused_computation.44 | convolution fusion | flops 2157969408 | bytes 6303744 | tf_op jit(solution)/shard_map/rd,dhc->rhc/dot_general | solution.py:25
  14.4 1.3 copy-done.2
  15.7 1.2 fusion.49
  17.6 12.9 %while.56 = (s32[]{:T(128)}, f32[1024,2,128]{0,2,1:T(8,128)}, s32[2]{0:T(128)S(1)}, bf16[1024,2,128]{0,2,1:T(8,128)(2,1)S(1)}, s32[24]{0:T(128)S(1)}, /*index=5*...) while((s32[]{:T(128)}, f32[1024,2,128]{0,2,1:T(8,128)}, ...), condition=%wide.region_6.7_spmd.clone.clone.clone, body=%wide.region_4.6_spmd.clone.clone.clone.sunk | while | flops 546871296 | bytes 4219704 | solution.py:66
  17.6 0.7 dynamic_slice.51
  19.1 0.6 and_and_fusion.4
  19.6 4.2 %fusion.65 = f32[1024,2,128]{0,2,1:T(8,128)} fusion(bf16[1024,2,128]{2,0,1:T(8,128)(2,1)} %get-tuple-element.781, pred[1024,512]{0,1:T(8,128)(4,1)S(1)} %and_and_fusion.4, f32[1024,2,128]{0,2,1:T(8,128)} %get-tuple-element.761, pred[]{:T(512)S(6)} %compare.5, bf16[1024,2,128]{2,0,1:T(8,128)(2,1)} %get-tuple-element.780, s32[]{:T(128)S(6)} %select_n.48, ...), kind=kOutput, calls=%fused_computation.33.clone.1 | convolution fusion | flops 544735232 | bytes 3671552 | tf_op jit(solution)/shard_map/while/body/eval_jaxpr/hrk,khc->rhc/dot_general | solution.py:61
  23.9 0.7 dynamic_slice.51
  25.9 4.6 %fusion.65 = f32[1024,2,128]{0,2,1:T(8,128)} fusion(bf16[1024,2,128]{2,0,1:T(8,128)(2,1)} %get-tuple-element.781, pred[1024,512]{0,1:T(8,128)(4,1)S(1)} %and_and_fusion.4, f32[1024,2,128]{0,2,1:T(8,128)} %get-tuple-element.761, pred[]{:T(512)S(6)} %compare.5, bf16[1024,2,128]{2,0,1:T(8,128)(2,1)} %get-tuple-element.780, s32[]{:T(128)S(6)} %select_n.48, ...), kind=kOutput, calls=%fused_computation.33.clone.1 | convolution fusion | flops 544735232 | bytes 3671552 | tf_op jit(solution)/shard_map/while/body/eval_jaxpr/hrk,khc->rhc/dot_general | solution.py:61
  30.5 64.3 %while.55 = (s32[]{:T(128)}, bf16[1024,2,128]{2,0,1:T(8,128)(2,1)}, bf16[1024,2,128]{0,2,1:T(8,128)(2,1)S(1)}, f32[1024,2,128]{0,2,1:T(8,128)}, s32[]{:T(128)}, ...) while((s32[]{:T(128)}, bf16[1024,2,128]{2,0,1:T(8,128)(2,1)}, ...), condition=%wide.region_11.12_spmd.clone.clone, body=%wide.region_7.11_spmd.clone.clone.sunk | while | flops 546609152 | bytes 10511020 | solution.py:82
  30.5 1.9 %collective-permute-start = (bf16[1024,2,128]{2,0,1:T(8,128)(2,1)}, bf16[1024,2,128]{2,0,1:T(8,128)(2,1)S(1)}, u32[]{:S(2)}, u32[]{:S(2)}) collective-permute-start(bf16[1024,2,128]{2,0,1:T(8,128)(2,1)} %get-tuple-element.802), channel_id=1, source_target_pairs={{0,4},{4,8},{8,12},{12,16},{16,20},{20,24},{24,28},{1,5},{5,9},{9,... | collective-permute-start | bytes 1572872 | tf_op jit(solution)/shard_map/while/body/eval_jaxpr/ppermute | solution.py:10
  32.4 3.5 %collective-permute-start.1 = (bf16[1024,2,128]{0,2,1:T(8,128)(2,1)S(1)}, bf16[1024,2,128]{0,2,1:T(8,128)(2,1)}, u32[]{:S(2)}, u32[]{:S(2)}) collective-permute-start(bf16[1024,2,128]{0,2,1:T(8,128)(2,1)S(1)} %get-tuple-element.803), channel_id=1, source_target_pairs={{0,4},{4,8},{8,12},{12,16},{16,20},{20,24},{24,28},{1,5},{5,9},{9,... | collective-permute-start | bytes 1572872 | tf_op jit(solution)/shard_map/while/body/eval_jaxpr/ppermute | solution.py:10
  35.9 6.2 %collective-permute-done = bf16[1024,2,128]{2,0,1:T(8,128)(2,1)S(1)} collective-permute-done((bf16[1024,2,128]{2,0,1:T(8,128)(2,1)}, bf16[1024,2,128]{2,0,1:T(8,128)(2,1)S(1)}, u32[]{:S(2)}, u32[]{:S(2)}) %collective-permute-start) | collective-permute-done | bytes 524320 | tf_op jit(solution)/shard_map/while/body/eval_jaxpr/ppermute | solution.py:10
  42.1 5.7 %collective-permute-done.1 = bf16[1024,2,128]{0,2,1:T(8,128)(2,1)} collective-permute-done((bf16[1024,2,128]{0,2,1:T(8,128)(2,1)S(1)}, bf16[1024,2,128]{0,2,1:T(8,128)(2,1)}, u32[]{:S(2)}, u32[]{:S(2)}) %collective-permute-start.1) | collective-permute-done | bytes 524320 | tf_op jit(solution)/shard_map/while/body/eval_jaxpr/ppermute | solution.py:10
  47.8 13.0 %while.57 = (s32[]{:T(128)}, f32[1024,2,128]{0,2,1:T(8,128)}, s32[2]{0:T(128)S(1)}, bf16[1024,2,128]{0,2,1:T(8,128)(2,1)}, s32[24]{0:T(128)S(1)}, /*index=5*/s32...) while((s32[]{:T(128)}, f32[1024,2,128]{0,2,1:T(8,128)}, ...), condition=%wide.region_10.10_spmd, body=%wide.region_8.9_spmd.sunk | while | flops 546608128 | bytes 4215091 | solution.py:66
  47.8 0.6 dynamic_slice.54
  49.2 0.6 and_and_fusion.5
  49.7 4.6 %fusion.69 = f32[1024,2,128]{0,2,1:T(8,128)} fusion(f32[1024,2,128]{0,2,1:T(8,128)} %get-tuple-element.720, bf16[1024,2,128]{2,0,1:T(8,128)(2,1)} %get-tuple-element.742, pred[1024,512]{0,1:T(8,128)(4,1)S(1)} %and_and_fusion.5, bf16[1024,2,128]{2,0,1:T(8,128)(2,1)S(1)} %get-tuple-element.741, s32[]{:T(128)S(6)} %select_n.50, ...), kind=kOutput, calls=%fused_computation.12.clone.1 | convolution fusion | flops 544473088 | bytes 3671040 | tf_op jit(solution)/shard_map/while/body/eval_jaxpr/while/body/eval_jaxpr/hrk,khc->rhc/dot_general | solution.py:61
  54.3 0.6 dynamic_slice.54
  55.7 0.6 and_and_fusion.5
  56.2 4.6 %fusion.69 = f32[1024,2,128]{0,2,1:T(8,128)} fusion(f32[1024,2,128]{0,2,1:T(8,128)} %get-tuple-element.720, bf16[1024,2,128]{2,0,1:T(8,128)(2,1)} %get-tuple-element.742, pred[1024,512]{0,1:T(8,128)(4,1)S(1)} %and_and_fusion.5, bf16[1024,2,128]{2,0,1:T(8,128)(2,1)S(1)} %get-tuple-element.741, s32[]{:T(128)S(6)} %select_n.50, ...), kind=kOutput, calls=%fused_computation.12.clone.1 | convolution fusion | flops 544473088 | bytes 3671040 | tf_op jit(solution)/shard_map/while/body/eval_jaxpr/while/body/eval_jaxpr/hrk,khc->rhc/dot_general | solution.py:61
  60.8 0.8 copy.68
  61.6 1.0 copy.69
  62.7 1.9 %collective-permute-start = (bf16[1024,2,128]{2,0,1:T(8,128)(2,1)}, bf16[1024,2,128]{2,0,1:T(8,128)(2,1)S(1)}, u32[]{:S(2)}, u32[]{:S(2)}) collective-permute-start(bf16[1024,2,128]{2,0,1:T(8,128)(2,1)} %get-tuple-element.802), channel_id=1, source_target_pairs={{0,4},{4,8},{8,12},{12,16},{16,20},{20,24},{24,28},{1,5},{5,9},{9,... | collective-permute-start | bytes 1572872 | tf_op jit(solution)/shard_map/while/body/eval_jaxpr/ppermute | solution.py:10
  64.6 2.6 %collective-permute-start.1 = (bf16[1024,2,128]{0,2,1:T(8,128)(2,1)S(1)}, bf16[1024,2,128]{0,2,1:T(8,128)(2,1)}, u32[]{:S(2)}, u32[]{:S(2)}) collective-permute-start(bf16[1024,2,128]{0,2,1:T(8,128)(2,1)S(1)} %get-tuple-element.803), channel_id=1, source_target_pairs={{0,4},{4,8},{8,12},{12,16},{16,20},{20,24},{24,28},{1,5},{5,9},{9,... | collective-permute-start | bytes 1572872 | tf_op jit(solution)/shard_map/while/body/eval_jaxpr/ppermute | solution.py:10
  67.2 7.1 %collective-permute-done = bf16[1024,2,128]{2,0,1:T(8,128)(2,1)S(1)} collective-permute-done((bf16[1024,2,128]{2,0,1:T(8,128)(2,1)}, bf16[1024,2,128]{2,0,1:T(8,128)(2,1)S(1)}, u32[]{:S(2)}, u32[]{:S(2)}) %collective-permute-start) | collective-permute-done | bytes 524320 | tf_op jit(solution)/shard_map/while/body/eval_jaxpr/ppermute | solution.py:10
  74.2 5.7 %collective-permute-done.1 = bf16[1024,2,128]{0,2,1:T(8,128)(2,1)} collective-permute-done((bf16[1024,2,128]{0,2,1:T(8,128)(2,1)S(1)}, bf16[1024,2,128]{0,2,1:T(8,128)(2,1)}, u32[]{:S(2)}, u32[]{:S(2)}) %collective-permute-start.1) | collective-permute-done | bytes 524320 | tf_op jit(solution)/shard_map/while/body/eval_jaxpr/ppermute | solution.py:10
  80.0 13.0 %while.57 = (s32[]{:T(128)}, f32[1024,2,128]{0,2,1:T(8,128)}, s32[2]{0:T(128)S(1)}, bf16[1024,2,128]{0,2,1:T(8,128)(2,1)}, s32[24]{0:T(128)S(1)}, /*index=5*/s32...) while((s32[]{:T(128)}, f32[1024,2,128]{0,2,1:T(8,128)}, ...), condition=%wide.region_10.10_spmd, body=%wide.region_8.9_spmd.sunk | while | flops 546608128 | bytes 4215091 | solution.py:66
  80.0 0.6 dynamic_slice.54
  81.3 0.6 and_and_fusion.5
  81.9 4.6 %fusion.69 = f32[1024,2,128]{0,2,1:T(8,128)} fusion(f32[1024,2,128]{0,2,1:T(8,128)} %get-tuple-element.720, bf16[1024,2,128]{2,0,1:T(8,128)(2,1)} %get-tuple-element.742, pred[1024,512]{0,1:T(8,128)(4,1)S(1)} %and_and_fusion.5, bf16[1024,2,128]{2,0,1:T(8,128)(2,1)S(1)} %get-tuple-element.741, s32[]{:T(128)S(6)} %select_n.50, ...), kind=kOutput, calls=%fused_computation.12.clone.1 | convolution fusion | flops 544473088 | bytes 3671040 | tf_op jit(solution)/shard_map/while/body/eval_jaxpr/while/body/eval_jaxpr/hrk,khc->rhc/dot_general | solution.py:61
  86.5 0.6 dynamic_slice.54
  87.8 0.6 and_and_fusion.5
  88.4 4.6 %fusion.69 = f32[1024,2,128]{0,2,1:T(8,128)} fusion(f32[1024,2,128]{0,2,1:T(8,128)} %get-tuple-element.720, bf16[1024,2,128]{2,0,1:T(8,128)(2,1)} %get-tuple-element.742, pred[1024,512]{0,1:T(8,128)(4,1)S(1)} %and_and_fusion.5, bf16[1024,2,128]{2,0,1:T(8,128)(2,1)S(1)} %get-tuple-element.741, s32[]{:T(128)S(6)} %select_n.50, ...), kind=kOutput, calls=%fused_computation.12.clone.1 | convolution fusion | flops 544473088 | bytes 3671040 | tf_op jit(solution)/shard_map/while/body/eval_jaxpr/while/body/eval_jaxpr/hrk,khc->rhc/dot_general | solution.py:61
  93.0 0.8 copy.68
  93.8 1.0 copy.69
  94.8 1.6 copy.38
  96.4 1.3 reduce_sum.66
  97.7 0.6 multiply_reduce_fusion.1
  98.4 2.4 %multiply_convert_fusion.2 = bf16[1024,2,128]{2,0,1:T(8,128)(2,1)} fusion(f32[1024,2,128]{2,0,1:T(8,128)S(1)} %copy.38, bf16[1024,2,512]{2,0,1:T(8,128)(2,1)} %copy-done.2, f32[2,128]{1,0:T(2,128)S(1)} %copy-done.3, f32[1024,2]{0,1:T(2,128)S(1)} %add_rsqrt_fusion, f32[1024,2]{0,1:T(2,128)S(1)} %broadcast_multiply_fusion), kind=kLoop, calls=%fused_computation.57 | loop fusion | flops 1572864 | bytes 2114560 | tf_op jit(solution)/shard_map/convert_element_type | solution.py:91
  100.8 2.0 %copy.39 = bf16[2,128,1024]{1,0,2:T(2,128)(2,1)} copy(bf16[2,128,1024]{2,1,0:T(8,128)(2,1)} %param.17) | data formatting | bytes 1048576 | tf_op args[5]
  102.8 4.9 %all-to-all-start = ((bf16[2,128,1024]{1,0,2:T(2,128)(2,1)}), bf16[2,128,1024]{1,0,2:T(2,128)(2,1)S(1)}, u32[]{:S(2)}, u32[]{:S(2)}) async-start(bf16[2,128,1024]{1,0,2:T(2,128)(2,1)} %copy.39), calls=%async_computation | async-start | bytes 1048576 | tf_op jit(solution)/shard_map/all_to_all | solution.py:92
  107.6 4.1 %convert_element_type.33 = f32[1024,1024]{1,0:T(8,128)} convert(bf16[1024,1024]{1,0:T(8,128)(2,1)} %param.12) | non-fusion elementwise | flops 1048576 | bytes 6291456 | tf_op jit(solution)/shard_map/convert_element_type | solution.py:21
  111.8 22.0 %all-to-all-done = bf16[2,128,1024]{1,0,2:T(2,128)(2,1)S(1)} async-done(((bf16[2,128,1024]{1,0,2:T(2,128)(2,1)}), bf16[2,128,1024]{1,0,2:T(2,128)(2,1)S(1)}, u32[]{:S(2)}, u32[]{:S(2)}) %all-to-all-start) | async-done | bytes 524320 | tf_op jit(solution)/shard_map/all_to_all | solution.py:92
  134.1 19.7 %all-gather.2.cloned.1.call-done = bf16[1024,8,128]{2,0,1:T(8,128)(2,1)} async-done(((bf16[1024,2,128]{2,0,1:T(8,128)(2,1)}), bf16[1024,8,128]{2,0,1:T(8,128)(2,1)}) %all-gather.2.cloned.1.call-update) | async-done | bytes 2097168 | tf_op jit(solution)/shard_map/all_gather | solution.py:95
  153.8 3.4 %fusion.48 = bf16[1024,256]{1,0:T(8,128)(2,1)} fusion(bf16[1024,8,128]{2,0,1:T(8,128)(2,1)} %all-gather.2.cloned.1.call-done, bf16[8,128,256]{2,1,0:T(8,128)(2,1)S(1)} %bitcast.89, f32[1024,1024]{1,0:T(8,128)} %convert_element_type.33, s32[]{:T(128)S(6)} %select_n.18), kind=kOutput, calls=%fused_computation.56 | convolution fusion | flops 537395200 | bytes 4194308 | tf_op jit(solution)/shard_map/rhc,hcd->rd/dot_general | solution.py:93
  (51 shorter events, 2.2 us)
Async XLA Ops:
  6.5 4.4 %copy-start = (bf16[1024,2,512]{2,1,0:T(2,128)(2,1)S(1)}, bf16[1024,2,512]{2,1,0:T(2,128)(2,1)}, u32[]{:S(2)}) copy-start(bf16[1024,2,512]{2,1,0:T(2,128)(2,1)} %param.15) | copy-start | bytes 6291460
  6.5 4.4 %copy-start.5 = (f32[1024]{0:T(1024)S(1)}, f32[1024]{0:T(1024)}, u32[]{:S(2)}) copy-start(f32[1024]{0:T(1024)} %param.14) | copy-start | bytes 12292
  6.5 147.3 %all-gather.2.cloned.1.call-start = ((), (), s32[]{:S(2)}) async-start(), calls=%async_computation.1 | async-start | bytes 2621440 | tf_op jit(solution)/shard_map/all_gather | solution.py:95
  6.5 4.4 %copy-start.1 = (bf16[1024,1024]{1,0:T(8,128)(2,1)S(1)}, bf16[1024,1024]{1,0:T(8,128)(2,1)}, u32[]{:S(2)}) copy-start(bf16[1024,1024]{1,0:T(8,128)(2,1)} %param.12) | copy-start | bytes 6291460
  14.4 1.4 copy-start.2
  15.7 1.5 copy-start.4
  30.5 11.6 %collective-permute-start = (bf16[1024,2,128]{2,0,1:T(8,128)(2,1)}, bf16[1024,2,128]{2,0,1:T(8,128)(2,1)S(1)}, u32[]{:S(2)}, u32[]{:S(2)}) collective-permute-start(bf16[1024,2,128]{2,0,1:T(8,128)(2,1)} %get-tuple-element.802), channel_id=1, source_target_pairs={{0,4},{4,8},{8,12},{12,16},{16,20},{20,24},{24,28},{1,5},{5,9},{9,... | collective-permute-start | bytes 1572872 | tf_op jit(solution)/shard_map/while/body/eval_jaxpr/ppermute | solution.py:10
  32.4 15.4 %collective-permute-start.1 = (bf16[1024,2,128]{0,2,1:T(8,128)(2,1)S(1)}, bf16[1024,2,128]{0,2,1:T(8,128)(2,1)}, u32[]{:S(2)}, u32[]{:S(2)}) collective-permute-start(bf16[1024,2,128]{0,2,1:T(8,128)(2,1)S(1)} %get-tuple-element.803), channel_id=1, source_target_pairs={{0,4},{4,8},{8,12},{12,16},{16,20},{20,24},{24,28},{1,5},{5,9},{9,... | collective-permute-start | bytes 1572872 | tf_op jit(solution)/shard_map/while/body/eval_jaxpr/ppermute | solution.py:10
  62.7 11.6 %collective-permute-start = (bf16[1024,2,128]{2,0,1:T(8,128)(2,1)}, bf16[1024,2,128]{2,0,1:T(8,128)(2,1)S(1)}, u32[]{:S(2)}, u32[]{:S(2)}) collective-permute-start(bf16[1024,2,128]{2,0,1:T(8,128)(2,1)} %get-tuple-element.802), channel_id=1, source_target_pairs={{0,4},{4,8},{8,12},{12,16},{16,20},{20,24},{24,28},{1,5},{5,9},{9,... | collective-permute-start | bytes 1572872 | tf_op jit(solution)/shard_map/while/body/eval_jaxpr/ppermute | solution.py:10
  64.6 15.4 %collective-permute-start.1 = (bf16[1024,2,128]{0,2,1:T(8,128)(2,1)S(1)}, bf16[1024,2,128]{0,2,1:T(8,128)(2,1)}, u32[]{:S(2)}, u32[]{:S(2)}) collective-permute-start(bf16[1024,2,128]{0,2,1:T(8,128)(2,1)S(1)} %get-tuple-element.803), channel_id=1, source_target_pairs={{0,4},{4,8},{8,12},{12,16},{16,20},{20,24},{24,28},{1,5},{5,9},{9,... | collective-permute-start | bytes 1572872 | tf_op jit(solution)/shard_map/while/body/eval_jaxpr/ppermute | solution.py:10
  94.8 3.6 %copy-start.3 = (f32[2,128]{1,0:T(2,128)S(1)}, f32[2,128]{1,0:T(2,128)}, u32[]{:S(2)}) copy-start(f32[2,128]{1,0:T(2,128)} %param.16) | copy-start | bytes 3076
  102.8 31.0 %all-to-all-start = ((bf16[2,128,1024]{1,0,2:T(2,128)(2,1)}), bf16[2,128,1024]{1,0,2:T(2,128)(2,1)S(1)}, u32[]{:S(2)}, u32[]{:S(2)}) async-start(bf16[2,128,1024]{1,0,2:T(2,128)(2,1)} %copy.39), calls=%async_computation | async-start | bytes 1048576 | tf_op jit(solution)/shard_map/all_to_all | solution.py:92
Sparse Core Ops, SparseCore 0:
  100.9 52.8 all-gather.1
where the time goes:
time: 166 us; the launch traced here: 164 us
  waiting for transfers between devices  66.4 us (40%)
  matrix products  33.8 us (20%)
  other arithmetic  17 us (10%)
  starting transfers between devices  14.8 us (9%)
  local copies, waits for them, and re-layouts  14.2 us (9%)
  between operations  13.5 us (8%)
  loops' own time  4.27 us (3%)
    dot_general x6, matrix products, block_step(): jnp.einsum('hrk,khc->rhc', weights, value_block, preferred_element_type=j...  27.1 us
    ppermute x4, waiting for transfers between devices, from_behind(): lax.ppermute(value, axis, [(source, source + steps) for source in range(i...  24.7 us
    all_to_all x1, waiting for transfers between devices, on_device(): lax.all_to_all(w_out, 'narrow', split_axis=2, concat_axis=0, tiled=True)  22 us
    all_gather x1, waiting for transfers between devices, on_device(): lax.all_gather(gated, 'narrow', axis=1, tiled=True)  19.7 us
    ppermute x4, starting transfers between devices, from_behind(): lax.ppermute(value, axis, [(source, source + steps) for source in range(i...  9.92 us
    all_to_all x1, starting transfers between devices, on_device(): lax.all_to_all(w_out, 'narrow', split_axis=2, concat_axis=0, tiled=True)  4.87 us
    another operation x3, loops' own time, attend(): lax.scan(block_step, running, jnp.arange(key_count // block_rows, dtype=j...  4.21 us
    convert_element_type x1, other arithmetic, on_device(): events_f = events.astype(jnp.float32)  4.11 us
  transfers between devices with their start and end apart: 6, of which 6 were waited for; matrix products, arithmetic and copies ran while one was open for 4% of the time, Pallas kernels for 0%

commit v1 on v0

v1 whole, which is shorter than its diff:
```python
import functools

import jax
import jax.numpy as jnp
from jax import lax
from jax.experimental import pallas as pl
from jax.experimental.pallas import tpu as pltpu
from jax.sharding import PartitionSpec as P

MESH = pl.DeviceIdType.MESH
F32 = jnp.float32
BF16 = jnp.bfloat16


def half_silu(half):
    return half + half * jnp.tanh(half)


def kernel(
    wide, narrow, reach, parts,
    len_ref, ev_ref, gain_ref, w_ref, og_ref, wo_ref, out_ref,
    normed, ubuf, qbuf, kvbuf, acc, start_ref, gown, gbuf, wcols, oacc,
    kv_send, kv_recv, g_send, g_recv, w_send, w_recv,
):
    me_w = lax.axis_index("wide")
    me_z = lax.axis_index("narrow")
    rows, width = ev_ref.shape
    heads, size = og_ref.shape
    share = out_ref.shape[1]
    users = len_ref.shape[0]
    tile = min(256, rows)
    tiles = rows // tile
    part = rows // parts

    barrier = pltpu.get_barrier_semaphore()

    @pl.when(me_w > 0)
    def _():
        pl.semaphore_signal(barrier, inc=1, device_id=(me_w - 1, me_z), device_id_type=MESH)

    @pl.when(me_w < wide - 1)
    def _():
        pl.semaphore_signal(barrier, inc=1, device_id=(me_w + 1, me_z), device_id_type=MESH)

    for d in range(1, narrow):
        @pl.when(me_z + d < narrow)
        def _():
            pl.semaphore_signal(barrier, inc=1, device_id=(me_w, me_z + d), device_id_type=MESH)

        @pl.when(me_z - d >= 0)
        def _():
            pl.semaphore_signal(barrier, inc=1, device_id=(me_w, me_z - d), device_id_type=MESH)

    def w_copy(direction, d):
        peer = me_z + d if direction == 0 else me_z - d
        return pltpu.make_async_remote_copy(
            src_ref=wo_ref.at[:, pl.ds(pl.multiple_of(peer * share, share), share)],
            dst_ref=wcols.at[direction, d - 1],
            send_sem=w_send.at[direction, d - 1],
            recv_sem=w_recv.at[direction, d - 1],
            device_id=(me_w, peer),
            device_id_type=MESH,
        )

    def w_landed(direction, d):
        return pltpu.make_async_remote_copy(
            src_ref=wcols.at[direction, d - 1],
            dst_ref=wcols.at[direction, d - 1],
            send_sem=w_send.at[direction, d - 1],
            recv_sem=w_recv.at[direction, d - 1],
            device_id=(me_w, me_z),
            device_id_type=MESH,
        )

    def kv_copy(step, h):
        return pltpu.make_async_remote_copy(
            src_ref=kvbuf.at[step - 1, h],
            dst_ref=kvbuf.at[step, h],
            send_sem=kv_send.at[step - 1, h],
            recv_sem=kv_recv.at[step - 1, h],
            device_id=(me_w + 1, me_z),
            device_id_type=MESH,
        )

    def kv_goes(step):
        return (me_w >= step - 1) & (me_w < wide - 1)

    def kv_start(step, h):
        @pl.when(kv_goes(step))
        def _():
            kv_copy(step, h).start()

    def g_copy(direction, d, c):
        h, r = c // parts, c % parts
        rs = pl.ds(r * part, part)
        src = gown.at[h, rs] if d == 1 else gbuf.at[direction, d - 2, h, rs]
        peer = me_z + 1 if direction == 0 else me_z - 1
        return pltpu.make_async_remote_copy(
            src_ref=src,
            dst_ref=gbuf.at[direction, d - 1, h, rs],
            send_sem=g_send.at[direction, d - 1, c],
            recv_sem=g_recv.at[direction, d - 1, c],
            device_id=(me_w, peer),
            device_id_type=MESH,
        )

    def g_goes(direction, d):
        if direction == 0:
            return (me_z >= d - 1) & (me_z < narrow - 1)
        return (me_z + d - 1 < narrow) & (me_z > 0)

    def g_start(direction, d, c):
        @pl.when(g_goes(direction, d))
        def _():
            g_copy(direction, d, c).start()

    def has(direction, d):
        return me_z >= d if direction == 0 else me_z + d < narrow

    ln_tile = min(128, rows)

    def ln(t, _):
        rs = pl.ds(pl.multiple_of(t * ln_tile, ln_tile), ln_tile)
        x = ev_ref[rs, :].astype(F32)
        x = x - jnp.mean(x, axis=1, keepdims=True)
        var = jnp.mean(x * x, axis=1, keepdims=True)
        normed[rs, :] = (x * lax.rsqrt(var + 1e-5) * gain_ref[...]).astype(BF16)
        return 0

    lax.fori_loop(0, rows // ln_tile, ln, 0)

    def project(h):
        def body(t, _):
            rs = pl.ds(pl.multiple_of(t * tile, tile), tile)
            p = jnp.dot(
                normed[rs, :], w_ref[:, h * 4 * size:(h + 1) * 4 * size],
                preferred_element_type=F32,
            )
            p = half_silu(p * 0.5).astype(BF16)
            ubuf[h, rs, :] = p[:, :size]
            kvbuf[0, h, 1, rs, :] = p[:, size:2 * size]
            qbuf[h, rs, :] = p[:, 2 * size:3 * size]
            kvbuf[0, h, 0, rs, :] = p[:, 3 * size:]
            return 0

        lax.fori_loop(0, tiles, body, 0)

    project(0)

    greeted = (
        jnp.where(me_w > 0, 1, 0) + jnp.where(me_w < wide - 1, 1, 0) + (narrow - 1)
    )
    pl.semaphore_wait(barrier, greeted)
    kv_start(1, 0)
    for d in range(1, narrow):
        @pl.when(me_z + d < narrow)
        def _():
            w_copy(0, d).start()

        @pl.when(me_z - d >= 0)
        def _():
            w_copy(1, d).start()

    for h in range(1, heads):
        project(h)

    lane = lax.broadcasted_iota(jnp.int32, (8, 128), 1)
    ends = jnp.zeros((8, 128), jnp.int32)
    for u in range(users):
        ends = ends + jnp.where(lane >= u, len_ref[u], 0)
    ends = jnp.where(lane < users, ends, jnp.int32(2 ** 30))[:1]
    first = me_w * rows

    def starts(t, _):
        rs = pl.ds(pl.multiple_of(t * tile, tile), tile)
        at = first + t * tile + lax.broadcasted_iota(jnp.int32, (tile, 128), 0)
        begun = jnp.max(jnp.where(ends <= at, ends, 0), axis=1, keepdims=True)
        start_ref[rs, :] = jnp.broadcast_to(begun - first, (tile, 128))
        return 0

    lax.fori_loop(0, tiles, starts, 0)
    scale = 0.5 * size ** (-0.5)

    def attend(step, h, lo=0, hi=None):
        def body(t, _):
            rs = pl.ds(pl.multiple_of(t * tile, tile), tile)
            s = lax.dot_general(
                qbuf[h, rs, :], kvbuf[step, h, 0],
                (((1,), (1,)), ((), ())), preferred_element_type=F32,
            )
            weights = half_silu(s * scale)
            key = lax.broadcasted_iota(jnp.int32, (1, rows), 1) - step * rows
            begun = start_ref[rs, :][:, :1]
            allowed = key >= begun
            if step == 0:
                query = t * tile + lax.broadcasted_iota(jnp.int32, (tile, 1), 0)
                allowed = allowed & (key <= query)
            weights = jnp.where(allowed, weights, 0.0).astype(BF16)
            out = jnp.dot(weights, kvbuf[step, h, 1], preferred_element_type=F32)
            if step == 0:
                acc[h, rs, :] = out
            else:
                acc[h, rs, :] += out
            return 0

        lax.fori_loop(lo, tiles if hi is None else hi, body, 0)

    def attend_far(step, h, lo=0, hi=None):
        @pl.when(me_w >= step)
        def _():
            attend(step, h, lo, hi)

    def kv_wait(step, h):
        @pl.when(me_w >= step)
        def _():
            kv_copy(step, h).wait_recv()

    def gate(h, lo, hi):
        def body(t, _):
            rs = pl.ds(pl.multiple_of(t * tile, tile), tile)
            a = acc[h, rs, :]
            a = a - jnp.mean(a, axis=1, keepdims=True)
            var = jnp.mean(a * a, axis=1, keepdims=True)
            g = a * lax.rsqrt(var + 1e-5) * og_ref[h:h + 1, :]
            gown[h, rs, :] = (g * ubuf[h, rs, :].astype(F32)).astype(BF16)
            return 0

        lax.fori_loop(lo, hi, body, 0)

    def finish(h):
        per = tiles // parts
        for r in range(parts):
            attend_far(reach, h, r * per, (r + 1) * per)
            gate(h, r * per, (r + 1) * per)
            for direction in range(2):
                g_start(direction, 1, h * parts + r)

    def own_cols(t):
        rs = pl.ds(pl.multiple_of(t * tile, tile), tile)
        cols = pl.ds(pl.multiple_of(me_z * share, share), share)
        return rs, cols

    kv_wait(1, 0)
    for step in range(2, min(reach, 2) + 1):
        kv_start(step, 0)
    for h in range(1, heads):
        kv_start(1, h)
    for h in range(heads):
        attend(0, h)
    attend_far(1, 0)
    for step in range(2, reach + 1):
        kv_wait(step, 0)
        if step < reach:
            kv_start(step + 1, 0)
        if step == 2:
            for h in range(1, heads):
                kv_wait(1, h)
                kv_start(2, h)
        if step < reach:
            attend_far(step, 0)

    def residual(t, _):
        rs, cols = own_cols(t)
        oacc[rs, :] = ev_ref[rs, cols].astype(F32)
        return 0

    finish(0)
    lax.fori_loop(0, tiles, residual, 0)
    for d in range(1, narrow):
        for direction in range(2):
            @pl.when(has(direction, d))
            def _():
                w_landed(direction, d).wait_recv()

    def relay(d, c):
        for direction in range(2):
            @pl.when(has(direction, d))
            def _():
                g_copy(direction, d, c).wait_recv()
            if d < narrow - 1:
                g_start(direction, d + 1, c)

    def gather_mul(d, c):
        h, r = c // parts, c % parts
        for direction in range(2):
            @pl.when(has(direction, d))
            def _():
                rs = pl.ds(r * part, part)
                oacc[rs, :] += jnp.dot(
                    gbuf[direction, d - 1, h, rs, :],
                    wcols[direction, d - 1, h * size:(h + 1) * size, :],
                    preferred_element_type=F32,
                )

    def own_mul(h):
        def body(t, _):
            rs, cols = own_cols(t)
            oacc[rs, :] += jnp.dot(
                gown[h, rs, :], wo_ref[h * size:(h + 1) * size, cols],
                preferred_element_type=F32,
            )
            return 0

        lax.fori_loop(0, tiles, body, 0)

    own_mul(0)
    done = set()
    for h in range(1, heads):
        attend_far(1, h)
        for c in range((h - 1) * parts, h * parts):
            relay(1, c)
            gather_mul(1, c)
            done.add((1, c))
        for step in range(2, reach + 1):
            kv_wait(step, h)
            if step < reach:
                kv_start(step + 1, h)
                attend_far(step, h)
        finish(h)
        own_mul(h)
    left = [
        (d * parts + c, d, c)
        for d in range(1, narrow) for c in range(heads * parts) if (d, c) not in done
    ]
    for _, d, c in sorted(left):
        relay(d, c)
        gather_mul(d, c)

    def store(t, _):
        rs = pl.ds(pl.multiple_of(t * tile, tile), tile)
        out_ref[rs, :] = oacc[rs, :].astype(out_ref.dtype)
        return 0

    lax.fori_loop(0, tiles, store, 0)

    for step in range(1, reach + 1):
        @pl.when(kv_goes(step))
        def _():
            for h in range(heads):
                kv_copy(step, h).wait_send()
    for d in range(1, narrow):
        @pl.when(me_z + d < narrow)
        def _():
            w_copy(0, d).wait_send()

        @pl.when(me_z - d >= 0)
        def _():
            w_copy(1, d).wait_send()

        for direction in range(2):
            @pl.when(g_goes(direction, d))
            def _():
                for c in range(heads * parts):
                    g_copy(direction, d, c).wait_send()


def solution(mesh):
    wide, narrow = mesh.shape["wide"], mesh.shape["narrow"]
    reach = wide // 4
    parts = 2

    def on_device(events, lengths, in_gain, w_uvqk, out_gain, w_out):
        rows, width = events.shape
        heads, size = out_gain.shape
        share = w_out.shape[2] // narrow
        chunks = heads * parts
        vmem = pl.BlockSpec(memory_space=pltpu.VMEM)
        return pl.pallas_call(
            functools.partial(kernel, wide, narrow, reach, parts),
            out_shape=jax.ShapeDtypeStruct((rows, share), BF16),
            in_specs=[pl.BlockSpec(memory_space=pltpu.SMEM)] + [vmem] * 5,
            out_specs=vmem,
            scratch_shapes=[
                pltpu.VMEM((rows, width), BF16),
                pltpu.VMEM((heads, rows, size), BF16),
                pltpu.VMEM((heads, rows, size), BF16),
                pltpu.VMEM((reach + 1, heads, 2, rows, size), BF16),
                pltpu.VMEM((heads, rows, size), F32),
                pltpu.VMEM((rows, 128), jnp.int32),
                pltpu.VMEM((heads, rows, size), BF16),
                pltpu.VMEM((2, narrow - 1, heads, rows, size), BF16),
                pltpu.VMEM((2, narrow - 1, heads * size, share), BF16),
                pltpu.VMEM((rows, share), F32),
                pltpu.SemaphoreType.DMA((reach, heads)),
                pltpu.SemaphoreType.DMA((reach, heads)),
                pltpu.SemaphoreType.DMA((2, narrow - 1, chunks)),
                pltpu.SemaphoreType.DMA((2, narrow - 1, chunks)),
                pltpu.SemaphoreType.DMA((2, narrow - 1)),
                pltpu.SemaphoreType.DMA((2, narrow - 1)),
            ],
            compiler_params=pltpu.CompilerParams(
                collective_id=0, has_side_effects=True,
                vmem_limit_bytes=60 * 1024 * 1024,
            ),
        )(
            lengths, events, in_gain.reshape(1, width),
            w_uvqk.reshape(width, heads * 4 * size), out_gain,
            w_out.reshape(heads * size, w_out.shape[2]),
        )

    in_specs = (
        P("wide", None),
        P(),
        P(),
        P(None, "narrow", None),
        P("narrow", None),
        P("narrow", None, None),
    )
    return jax.shard_map(
        on_device, mesh=mesh, in_specs=in_specs, out_specs=P("wide", "narrow"), check_vma=False
    )
```

time: 166 us -> 65.3 us (0.39); the launches traced: 164 us -> 65.1 us
  waiting for transfers between devices: 66.4 us -> 0 us
  Pallas kernels: 0 us -> 59.7 us
  matrix products: 33.8 us -> 0 us
  other arithmetic: 17 us -> 0 us
  starting transfers between devices: 14.8 us -> 0 us
  between operations: 13.5 us -> 0.01 us
  local copies, waits for them, and re-layouts: 14.2 us -> 5.38 us
  loops' own time: 4.27 us -> 0 us
    pallas_call x0 -> x1, Pallas kernels: none -> 59.7 us  [on_device(): pl.pallas_call(functools.partial(kernel, wide, narrow, reach, parts), out...]
    dot_general x8 -> x0, matrix products: 33.8 us -> none  [the longest x6 27.1 us: block_step(): jnp.einsum('hrk,khc->rhc', weights, value_block, preferred_element_type=j...]
    ppermute x4 -> x0, waiting for transfers between devices: 24.7 us -> none  [from_behind(): lax.ppermute(value, axis, [(source, source + steps) for source in range(i...]
    all_to_all x1 -> x0, waiting for transfers between devices: 22 us -> none  [on_device(): lax.all_to_all(w_out, 'narrow', split_axis=2, concat_axis=0, tiled=True)]
    all_gather x1 -> x0, waiting for transfers between devices: 19.7 us -> none  [on_device(): lax.all_gather(gated, 'narrow', axis=1, tiled=True)]
    ppermute x4 -> x0, starting transfers between devices: 9.92 us -> none  [from_behind(): lax.ppermute(value, axis, [(source, source + steps) for source in range(i...]
    reduce_sum x11 -> x0, other arithmetic: 6.93 us -> none  [the longest x1 2.28 us: on_device(): variance = jnp.mean((events_f - average) ** 2, axis=-1, keepdims=True)]
    convert_element_type x2 -> x0, other arithmetic: 6.47 us -> none  [the longest x1 4.11 us: on_device(): events_f = events.astype(jnp.float32)]
  transfers between devices with their start and end apart: 6 -> 0, of which waited for: 6 -> 0; matrix products, arithmetic and copies ran while one was open for 4% -> 0% of each run, Pallas kernels for 0% -> 0%
where the time goes in v1:
time: 65.3 us; the launch traced here: 65.1 us
  Pallas kernels  59.7 us (91%)
  local copies, waits for them, and re-layouts  5.38 us (8%)
    pallas_call x1, Pallas kernels, on_device(): pl.pallas_call(functools.partial(kernel, wide, narrow, reach, parts), out...  59.7 us
    unnamed x2, local copies, waits for them, and re-layouts  5.38 us

profile of v1, /device:TPU:4, one launch (start us, length us, event | category | flops | bytes accessed | tf_op | source)
XLA Modules:
  0.0 65.1 jit_solution(13819695235969559830)
XLA Ops:
  0.0 3.5 %copy.7 = bf16[128,8,2,512]{3,1,2,0:T(8,128)(2,1)} copy(bf16[128,8,2,512]{3,2,1,0:T(2,128)(2,1)} %bitcast.5) | data formatting | bytes 4194304
  3.5 59.7 %shard_map.64 = bf16[1024,256]{1,0:T(8,128)(2,1)} custom-call(s32[24]{0:T(128)} %len_ref.1, bf16[1024,1024]{1,0:T(8,128)(2,1)} %ev_ref.1, f32[1,1024]{1,0:T(1,128)} %bitcast.7, bf16[1024,1024]{1,0:T(8,128)(2,1)} %bitcast.4, f32[2,128]{1,0:T(2,128)} %og_ref.1, bf16[256,1024]{1,0:T(8,128)(2,1)} %bitcast.6), custom_call_target="tpu_custom_call" | custom-call | tf_op jit(solution)/shard_map/pallas_call | solution.py:368
  63.3 1.9 %copy.9 = bf16[1024,256]{1,0:T(8,128)(2,1)} copy(bf16[1024,256]{1,0:T(8,128)(2,1)} %shard_map.64) | data formatting | bytes 1048576
